TPU v7x, 32 devices: a whole 2x2x4 slice. The times are simulated.
32 devices in a mesh: row: 8 (over y, x, core), col: 4 (over z).
Axes of the slice: x: 2, y: 2, z: 4, core: 2. Of those that a mesh axis runs over, the one named last changes fastest.
Arguments:
- layer_input: bfloat16 [8192, 1536], P(('row', 'col')), may hold values from -6 to 6
- context: bfloat16 [8, 130, 768], P('row'), may hold values from -6 to 6
- first_gain: float32 [1536], replicated, may hold values from 0.5 to 1.5
- query_weight: bfloat16 [1536, 1536], P('row', 'col'), may hold values from -0.15625 to 0.15625
- key_weight: bfloat16 [1536, 1536], P('row', 'col'), may hold values from -0.15625 to 0.15625
- value_weight: bfloat16 [1536, 1536], P('row', 'col'), may hold values from -0.15625 to 0.15625
- out_weight: bfloat16 [1536, 1536], P(('col', 'row')), may hold values from -3 to 3
- second_gain: float32 [1536], replicated, may hold values from 0.5 to 1.5
- cross_query: bfloat16 [1536, 1536], P('row', 'col'), may hold values from -0.15625 to 0.15625
- cross_key: bfloat16 [768, 1536], P('row', 'col'), may hold values from -0.21875 to 0.21875
- cross_value: bfloat16 [768, 1536], P('row', 'col'), may hold values from -0.21875 to 0.21875
- cross_out: bfloat16 [1536, 1536], P(('col', 'row')), may hold values from -1 to 1
- third_gain: float32 [1536], replicated, may hold values from 0.5 to 1.5
- gate_weight: bfloat16 [1536, 6144], P('row', 'col'), may hold values from -0.15625 to 0.15625
- up_weight: bfloat16 [1536, 6144], P('row', 'col'), may hold values from -0.15625 to 0.15625
- gate_bias: float32 [6144], P('col'), may hold values from -3 to 3
- up_bias: float32 [6144], P('col'), may hold values from -3 to 3
- down_weight: bfloat16 [6144, 1536], P(('col', 'row')), may hold values from -0.078125 to 0.078125
- down_bias: float32 [1536], replicated, may hold values from -3 to 3
- out_grad: bfloat16 [8192, 1536], P(('row', 'col')), may hold values from -6 to 6
Outputs:
- output: bfloat16 [8192, 1536], P(('row', 'col'))
- input_grad: float32 [8192, 1536], P(('row', 'col'))
- context_grad: float32 [8, 130, 768], P('row')
- first_gain_grad: float32 [1536], replicated
- query_grad: float32 [1536, 1536], P('row', 'col')
- key_grad: float32 [1536, 1536], P('row', 'col')
- value_grad: float32 [1536, 1536], P('row', 'col')
- out_weight_grad: float32 [1536, 1536], P(('col', 'row'))
- second_gain_grad: float32 [1536], replicated
- cross_query_grad: float32 [1536, 1536], P('row', 'col')
- cross_key_grad: float32 [768, 1536], P('row', 'col')
- cross_value_grad: float32 [768, 1536], P('row', 'col')
- cross_out_grad: float32 [1536, 1536], P(('col', 'row'))
- third_gain_grad: float32 [1536], replicated
- gate_grad: float32 [1536, 6144], P('row', 'col')
- up_grad: float32 [1536, 6144], P('row', 'col')
- gate_bias_grad: float32 [6144], P('col')
- up_bias_grad: float32 [6144], P('col')
- down_grad: float32 [6144, 1536], P(('col', 'row'))
- down_bias_grad: float32 [1536], replicated
All inputs are finite; a program needn't handle non-finite values.
Results may differ from a plain program's by a relative error of at most 0.024.
Values may be sent and summed in bfloat16 or wider, within the bound.
No kernel may reach another device: no remote copies, remote signals or barrier semaphores. Data moves between devices by JAX's collectives and lax.ppermute only.
A program may use at most 192 MiB of HBM per device.

v0:
```python
import jax
import jax.numpy as jnp
from jax import lax
from jax.sharding import PartitionSpec as P

HD = 64
LEN = 1024


norm_eps = 1e-05


def widen(narrow):
    return lax.all_gather(narrow, "col", axis=0, tiled=True)


def settle(partial_value):
    return lax.psum_scatter(partial_value, "col", scatter_dimension=0, tiled=True)


def mixed(left, right):
    return jnp.dot(left, right, preferred_element_type=jnp.float32)


def norm_forward(stream):
    average = jnp.mean(stream, axis=1, keepdims=True)
    centred = stream - average
    spread = jnp.mean(centred * centred, axis=1, keepdims=True)
    inverse = lax.rsqrt(spread + norm_eps)
    return (centred * inverse, inverse)


def norm_backward(grad_normed, normed, inverse, gain):
    scaled = grad_normed * gain
    first_mean = jnp.mean(scaled, axis=1, keepdims=True)
    second_mean = jnp.mean(scaled * normed, axis=1, keepdims=True)
    grad_stream = inverse * (scaled - first_mean - normed * second_mean)
    return (grad_stream, jnp.sum(grad_normed * normed, axis=0))


def rotary_tables(tokens):
    quarter = HD // 4
    freqs = 10000.0 ** (-jnp.arange(quarter, dtype=jnp.float32) / quarter)
    places = (jnp.arange(tokens, dtype=jnp.int32) % LEN).astype(jnp.float32)
    angles = places[:, None] * freqs[None, :]
    return (jnp.cos(angles)[:, None, :], jnp.sin(angles)[:, None, :])


def rotate(values, cosine, sine, direction):
    quarter = cosine.shape[-1]
    first = values[..., :quarter]
    second = values[..., quarter : 2 * quarter]
    return jnp.concatenate(
        [
            first * cosine - direction * second * sine,
            second * cosine + direction * first * sine,
            values[..., 2 * quarter :],
        ],
        axis=-1,
    )


def attention_forward(queries, keys, values, scale):
    block_len = min(512, LEN)
    heads = queries.shape[1]
    blocks = queries.shape[0] // block_len
    owners = jnp.arange(blocks, dtype=jnp.int32) // (LEN // block_len)

    def one_block(block_item):
        query, owner = block_item
        key_seq = lax.dynamic_index_in_dim(keys, owner, 0, keepdims=False)
        value_seq = lax.dynamic_index_in_dim(values, owner, 0, keepdims=False)
        scores = (
            jnp.einsum("qhd,khd->hqk", query, key_seq, preferred_element_type=jnp.float32) * scale
        )
        row_peak = jnp.max(scores, axis=-1, keepdims=True)
        lifted = jnp.exp(scores - row_peak)
        totals = jnp.sum(lifted, axis=-1, keepdims=True)
        probs = (lifted / totals).astype(jnp.bfloat16)
        result = jnp.einsum("hqk,khd->qhd", probs, value_seq, preferred_element_type=jnp.float32)
        return (result.astype(jnp.bfloat16), (row_peak + jnp.log(totals))[..., 0])

    outputs, logsum = lax.map(one_block, (queries.reshape(blocks, block_len, heads, HD), owners))
    return (outputs.reshape(queries.shape), logsum)


def attention_backward(queries, keys, values, grad_out, logsum, scale):
    block_len = min(512, LEN)
    heads = queries.shape[1]
    blocks = queries.shape[0] // block_len
    per_seq = LEN // block_len
    owners = jnp.arange(blocks, dtype=jnp.int32) // per_seq

    def one_block(block_item):
        query, grad_block, block_sum, owner = block_item
        key_seq = lax.dynamic_index_in_dim(keys, owner, 0, keepdims=False)
        value_seq = lax.dynamic_index_in_dim(values, owner, 0, keepdims=False)
        scores = (
            jnp.einsum("qhd,khd->hqk", query, key_seq, preferred_element_type=jnp.float32) * scale
        )
        probs = jnp.exp(scores - block_sum[..., None])
        grad_probs = jnp.einsum(
            "qhd,khd->hqk", grad_block, value_seq, preferred_element_type=jnp.float32
        )
        weighted = jnp.sum(grad_probs * probs, axis=-1, keepdims=True)
        grad_scores = (probs * (grad_probs - weighted)).astype(jnp.bfloat16)
        grad_query = (
            jnp.einsum("hqk,khd->qhd", grad_scores, key_seq, preferred_element_type=jnp.float32)
            * scale
        )
        grad_key = (
            jnp.einsum("hqk,qhd->khd", grad_scores, query, preferred_element_type=jnp.float32)
            * scale
        )
        grad_value = jnp.einsum(
            "hqk,qhd->khd",
            probs.astype(jnp.bfloat16),
            grad_block,
            preferred_element_type=jnp.float32,
        )
        return (grad_query, grad_key, grad_value)

    items = (
        queries.reshape(blocks, block_len, heads, HD),
        grad_out.reshape(blocks, block_len, heads, HD),
        logsum,
        owners,
    )
    grad_query, grad_key, grad_value = lax.map(one_block, items)
    seq_count = blocks // per_seq
    grad_key = jnp.sum(grad_key.reshape((seq_count, per_seq) + keys.shape[1:]), axis=1)
    grad_value = jnp.sum(grad_value.reshape((seq_count, per_seq) + values.shape[1:]), axis=1)
    return (grad_query.reshape(queries.shape), grad_key, grad_value)


def local(
    layer_input,
    context,
    first_gain,
    query_weight,
    key_weight,
    value_weight,
    out_weight,
    second_gain,
    cross_query,
    cross_key,
    cross_value,
    cross_out,
    third_gain,
    gate_weight,
    up_weight,
    gate_bias,
    up_bias,
    down_weight,
    down_bias,
    out_grad,
):
    (
        query_cols,
        key_cols,
        value_cols,
        cross_queries,
        cross_keys,
        cross_values,
        gate_cols,
        up_cols,
    ) = (
        lax.all_gather(query_weight, "row", axis=0, tiled=True),
        lax.all_gather(key_weight, "row", axis=0, tiled=True),
        lax.all_gather(value_weight, "row", axis=0, tiled=True),
        lax.all_gather(cross_query, "row", axis=0, tiled=True),
        lax.all_gather(cross_key, "row", axis=0, tiled=True),
        lax.all_gather(cross_value, "row", axis=0, tiled=True),
        lax.all_gather(gate_weight, "row", axis=0, tiled=True),
        lax.all_gather(up_weight, "row", axis=0, tiled=True),
    )
    out_rows, cross_rows, down_rows = (
        lax.all_gather(out_weight, "row", axis=0, tiled=True),
        lax.all_gather(cross_out, "row", axis=0, tiled=True),
        lax.all_gather(down_weight, "row", axis=0, tiled=True),
    )
    heads = query_cols.shape[1] // HD
    seq_count = context.shape[0]
    ctx_len = context.shape[1]
    tokens = seq_count * LEN
    scale = HD ** (-0.5)
    cosine, sine = rotary_tables(tokens)
    stream = layer_input.astype(jnp.float32)
    normed_one, inverse_one = norm_forward(stream)
    acts_one = widen((normed_one * first_gain).astype(jnp.bfloat16))
    self_queries = rotate(
        mixed(acts_one, query_cols).reshape(tokens, heads, HD), cosine, sine, 1.0
    ).astype(jnp.bfloat16)
    self_keys = rotate(
        mixed(acts_one, key_cols).reshape(tokens, heads, HD), cosine, sine, 1.0
    ).astype(jnp.bfloat16)
    self_keys = self_keys.reshape(seq_count, LEN, heads, HD)
    self_values = (
        mixed(acts_one, value_cols).astype(jnp.bfloat16).reshape(seq_count, LEN, heads, HD)
    )
    self_mixed, self_logsum = attention_forward(self_queries, self_keys, self_values, scale)
    self_flat = self_mixed.reshape(tokens, heads * HD)
    stream_one = stream + settle(mixed(self_flat, out_rows))
    normed_two, inverse_two = norm_forward(stream_one)
    acts_two = widen((normed_two * second_gain).astype(jnp.bfloat16))
    other_queries = mixed(acts_two, cross_queries).astype(jnp.bfloat16).reshape(tokens, heads, HD)
    other_keys = jnp.einsum(
        "sce,ef->scf", context, cross_keys, preferred_element_type=jnp.float32
    ).astype(jnp.bfloat16)
    other_values = jnp.einsum(
        "sce,ef->scf", context, cross_values, preferred_element_type=jnp.float32
    ).astype(jnp.bfloat16)
    other_keys = other_keys.reshape(seq_count, ctx_len, heads, HD)
    other_values = other_values.reshape(seq_count, ctx_len, heads, HD)
    other_mixed, other_logsum = attention_forward(other_queries, other_keys, other_values, scale)
    other_flat = other_mixed.reshape(tokens, heads * HD)
    stream_two = stream_one + settle(mixed(other_flat, cross_rows))
    normed_three, inverse_three = norm_forward(stream_two)
    acts_three = widen((normed_three * third_gain).astype(jnp.bfloat16))
    gate = mixed(acts_three, gate_cols) + gate_bias
    upward = mixed(acts_three, up_cols) + up_bias
    sigmoid_gate = jax.nn.sigmoid(gate)
    silu_gate = gate * sigmoid_gate
    hidden = (silu_gate * upward).astype(jnp.bfloat16)
    output_value = (stream_two + settle(mixed(hidden, down_rows)) + down_bias).astype(jnp.bfloat16)
    down_bias_part = jnp.sum(out_grad, axis=0, dtype=jnp.float32)
    grad_wide = widen(out_grad)
    down_part = jnp.einsum("tf,td->fd", hidden, grad_wide, preferred_element_type=jnp.float32)
    grad_hidden = jnp.einsum("td,fd->tf", grad_wide, down_rows, preferred_element_type=jnp.float32)
    grad_up = (grad_hidden * silu_gate).astype(jnp.bfloat16)
    grad_gate = (grad_hidden * upward * sigmoid_gate * (1.0 + gate * (1.0 - sigmoid_gate))).astype(
        jnp.bfloat16
    )
    gate_bias_part = jnp.sum(grad_gate, axis=0, dtype=jnp.float32)
    up_bias_part = jnp.sum(grad_up, axis=0, dtype=jnp.float32)
    gate_part = jnp.einsum("td,tf->df", acts_three, grad_gate, preferred_element_type=jnp.float32)
    up_part = jnp.einsum("td,tf->df", acts_three, grad_up, preferred_element_type=jnp.float32)
    grad_acts_three = settle(
        jnp.einsum("tf,df->td", grad_gate, gate_cols, preferred_element_type=jnp.float32)
        + jnp.einsum("tf,df->td", grad_up, up_cols, preferred_element_type=jnp.float32)
    )
    grad_norm_three, third_gain_part = norm_backward(
        grad_acts_three, normed_three, inverse_three, third_gain
    )
    grad_two = out_grad.astype(jnp.float32) + grad_norm_three
    grad_two_wide = widen(grad_two.astype(jnp.bfloat16))
    cross_out_part = jnp.einsum(
        "te,td->ed", other_flat, grad_two_wide, preferred_element_type=jnp.float32
    )
    grad_other = jnp.einsum(
        "td,ed->te", grad_two_wide, cross_rows, preferred_element_type=jnp.float32
    ).astype(jnp.bfloat16)
    grad_oq, grad_ok, grad_ov = attention_backward(
        other_queries,
        other_keys,
        other_values,
        grad_other.reshape(tokens, heads, HD),
        other_logsum,
        scale,
    )
    grad_oq = grad_oq.astype(jnp.bfloat16).reshape(tokens, heads * HD)
    grad_ok = grad_ok.astype(jnp.bfloat16).reshape(seq_count, ctx_len, heads * HD)
    grad_ov = grad_ov.astype(jnp.bfloat16).reshape(seq_count, ctx_len, heads * HD)
    cross_query_part = jnp.einsum(
        "td,te->de", acts_two, grad_oq, preferred_element_type=jnp.float32
    )
    cross_key_part = jnp.einsum("scf,sce->fe", context, grad_ok, preferred_element_type=jnp.float32)
    cross_value_part = jnp.einsum(
        "scf,sce->fe", context, grad_ov, preferred_element_type=jnp.float32
    )
    context_part = jnp.einsum(
        "sce,fe->scf", grad_ok, cross_keys, preferred_element_type=jnp.float32
    ) + jnp.einsum("sce,fe->scf", grad_ov, cross_values, preferred_element_type=jnp.float32)
    context_grad = lax.psum(context_part.astype(jnp.bfloat16), "col").astype(jnp.float32)
    grad_acts_two = settle(
        jnp.einsum("te,de->td", grad_oq, cross_queries, preferred_element_type=jnp.float32)
    )
    grad_norm_two, second_gain_part = norm_backward(
        grad_acts_two, normed_two, inverse_two, second_gain
    )
    grad_one = grad_two + grad_norm_two
    grad_one_wide = widen(grad_one.astype(jnp.bfloat16))
    out_weight_part = jnp.einsum(
        "te,td->ed", self_flat, grad_one_wide, preferred_element_type=jnp.float32
    )
    grad_self = jnp.einsum(
        "td,ed->te", grad_one_wide, out_rows, preferred_element_type=jnp.float32
    ).astype(jnp.bfloat16)
    grad_sq, grad_sk, grad_sv = attention_backward(
        self_queries,
        self_keys,
        self_values,
        grad_self.reshape(tokens, heads, HD),
        self_logsum,
        scale,
    )
    grad_sq = rotate(grad_sq, cosine, sine, -1.0).astype(jnp.bfloat16).reshape(tokens, heads * HD)
    grad_sk = (
        rotate(grad_sk.reshape(tokens, heads, HD), cosine, sine, -1.0)
        .astype(jnp.bfloat16)
        .reshape(tokens, heads * HD)
    )
    grad_sv = grad_sv.astype(jnp.bfloat16).reshape(tokens, heads * HD)
    query_part = jnp.einsum("td,te->de", acts_one, grad_sq, preferred_element_type=jnp.float32)
    key_part = jnp.einsum("td,te->de", acts_one, grad_sk, preferred_element_type=jnp.float32)
    value_part = jnp.einsum("td,te->de", acts_one, grad_sv, preferred_element_type=jnp.float32)
    grad_acts_one = settle(
        jnp.einsum("te,de->td", grad_sq, query_cols, preferred_element_type=jnp.float32)
        + jnp.einsum("te,de->td", grad_sk, key_cols, preferred_element_type=jnp.float32)
        + jnp.einsum("te,de->td", grad_sv, value_cols, preferred_element_type=jnp.float32)
    )
    grad_norm_one, first_gain_part = norm_backward(
        grad_acts_one, normed_one, inverse_one, first_gain
    )
    input_grad = grad_one + grad_norm_one
    (
        query_grad,
        key_grad,
        value_grad,
        cross_query_grad,
        cross_key_grad,
        cross_value_grad,
        gate_grad,
        up_grad,
    ) = (
        lax.psum_scatter(
            query_part.astype(jnp.bfloat16), "row", scatter_dimension=0, tiled=True
        ).astype(jnp.float32),
        lax.psum_scatter(
            key_part.astype(jnp.bfloat16), "row", scatter_dimension=0, tiled=True
        ).astype(jnp.float32),
        lax.psum_scatter(
            value_part.astype(jnp.bfloat16), "row", scatter_dimension=0, tiled=True
        ).astype(jnp.float32),
        lax.psum_scatter(
            cross_query_part.astype(jnp.bfloat16), "row", scatter_dimension=0, tiled=True
        ).astype(jnp.float32),
        lax.psum_scatter(
            cross_key_part.astype(jnp.bfloat16), "row", scatter_dimension=0, tiled=True
        ).astype(jnp.float32),
        lax.psum_scatter(
            cross_value_part.astype(jnp.bfloat16), "row", scatter_dimension=0, tiled=True
        ).astype(jnp.float32),
        lax.psum_scatter(
            gate_part.astype(jnp.bfloat16), "row", scatter_dimension=0, tiled=True
        ).astype(jnp.float32),
        lax.psum_scatter(
            up_part.astype(jnp.bfloat16), "row", scatter_dimension=0, tiled=True
        ).astype(jnp.float32),
    )
    out_weight_grad, cross_out_grad, down_grad = (
        lax.psum_scatter(
            out_weight_part.astype(jnp.bfloat16), "row", scatter_dimension=0, tiled=True
        ).astype(jnp.float32),
        lax.psum_scatter(
            cross_out_part.astype(jnp.bfloat16), "row", scatter_dimension=0, tiled=True
        ).astype(jnp.float32),
        lax.psum_scatter(
            down_part.astype(jnp.bfloat16), "row", scatter_dimension=0, tiled=True
        ).astype(jnp.float32),
    )
    gate_bias_grad, up_bias_grad = lax.psum((gate_bias_part, up_bias_part), "row")
    first_gain_grad, second_gain_grad, third_gain_grad, down_bias_grad = lax.psum(
        (first_gain_part, second_gain_part, third_gain_part, down_bias_part), ("row", "col")
    )
    return (
        output_value,
        input_grad,
        context_grad,
        first_gain_grad,
        query_grad,
        key_grad,
        value_grad,
        out_weight_grad,
        second_gain_grad,
        cross_query_grad,
        cross_key_grad,
        cross_value_grad,
        cross_out_grad,
        third_gain_grad,
        gate_grad,
        up_grad,
        gate_bias_grad,
        up_bias_grad,
        down_grad,
        down_bias_grad,
    )


def solution(mesh):
    in_specs = (
        P(("row", "col"), None),
        P("row", None, None),
        P(),
        P("row", "col"),
        P("row", "col"),
        P("row", "col"),
        P(("col", "row"), None),
        P(),
        P("row", "col"),
        P("row", "col"),
        P("row", "col"),
        P(("col", "row"), None),
        P(),
        P("row", "col"),
        P("row", "col"),
        P("col"),
        P("col"),
        P(("col", "row"), None),
        P(),
        P(("row", "col"), None),
    )
    out_specs = (
        P(("row", "col"), None),
        P(("row", "col"), None),
        P("row", None, None),
        P(),
        P("row", "col"),
        P("row", "col"),
        P("row", "col"),
        P(("col", "row"), None),
        P(),
        P("row", "col"),
        P("row", "col"),
        P("row", "col"),
        P(("col", "row"), None),
        P(),
        P("row", "col"),
        P("row", "col"),
        P("col"),
        P("col"),
        P(("col", "row"), None),
        P(),
    )
    return jax.shard_map(local, mesh=mesh, in_specs=in_specs, out_specs=out_specs, check_vma=False)
```

profile of v0, /device:TPU:0, one launch (start us, length us, event | category | flops | bytes accessed | tf_op | source)
XLA Modules:
  0.0 2001.6 jit_solution(11273441268996766799)
XLA Ops:
  36.6 65.6 %all-gather.16.cloned.1.call-done = bf16[1024,1536]{1,0:T(8,128)(2,1)} async-done(((bf16[256,1536]{1,0:T(8,128)(2,1)}), bf16[1024,1536]{1,0:T(8,128)(2,1)}) %all-gather.16.cloned.1.call-update) | async-done | bytes 3145744 | tf_op jit(solution)/shard_map/all_gather | solution.py:14
  185.0 109.9 %reduce-scatter.22.cloned.1.call-done = f32[256,1536]{1,0:T(8,128)} async-done(((f32[1024,1536]{1,0:T(8,128)}), f32[256,1536]{1,0:T(8,128)}) %reduce-scatter.22.cloned.1.call-update) | async-done | bytes 1572880 | tf_op jit(solution)/shard_map/reduce_scatter | solution.py:18
  323.6 65.0 %all-gather.26.cloned.1.call-done = bf16[1024,1536]{1,0:T(8,128)(2,1)} async-done(((bf16[256,1536]{1,0:T(8,128)(2,1)}), bf16[1024,1536]{1,0:T(8,128)(2,1)}) %all-gather.26.cloned.1.call-update) | async-done | bytes 3145744 | tf_op jit(solution)/shard_map/all_gather | solution.py:14
  419.9 110.1 %reduce-scatter.24.cloned.1.call-done = f32[256,1536]{1,0:T(8,128)} async-done(((f32[1024,1536]{1,0:T(8,128)}), f32[256,1536]{1,0:T(8,128)}) %reduce-scatter.24.cloned.1.call-update) | async-done | bytes 1572880 | tf_op jit(solution)/shard_map/reduce_scatter | solution.py:18
  536.3 35.0 %all-gather.36.cloned.1.call-done = bf16[1536,1536]{1,0:T(8,128)(2,1)} async-done(((bf16[192,1536]{1,0:T(8,128)(2,1)}), bf16[1536,1536]{1,0:T(8,128)(2,1)}) %all-gather.36.cloned.1.call-update) | async-done | bytes 4718608 | tf_op jit(solution)/shard_map/all_gather | solution.py:175
  571.3 65.5 %all-gather.32.cloned.1.call-done = bf16[1024,1536]{1,0:T(8,128)(2,1)} async-done(((bf16[256,1536]{1,0:T(8,128)(2,1)}), bf16[1024,1536]{1,0:T(8,128)(2,1)}) %all-gather.32.cloned.1.call-update) | async-done | bytes 3145744 | tf_op jit(solution)/shard_map/all_gather | solution.py:14
  685.8 55.2 %all-gather.40.cloned.1.call-done = bf16[1024,1536]{1,0:T(8,128)(2,1)} async-done(((bf16[256,1536]{1,0:T(8,128)(2,1)}), bf16[1024,1536]{1,0:T(8,128)(2,1)}) %all-gather.40.cloned.1.call-update) | async-done | bytes 3145744 | tf_op jit(solution)/shard_map/all_gather | solution.py:14
  741.0 39.2 %all-gather.38.cloned.1.call-done = bf16[1536,1536]{1,0:T(8,128)(2,1)} async-done(((bf16[192,1536]{1,0:T(8,128)(2,1)}), bf16[1536,1536]{1,0:T(8,128)(2,1)}) %all-gather.38.cloned.1.call-update) | async-done | bytes 4718608 | tf_op jit(solution)/shard_map/all_gather | solution.py:180
  819.9 100.6 %reduce-scatter.28.cloned.1.call-done = f32[256,1536]{1,0:T(8,128)} async-done(((f32[1024,1536]{1,0:T(8,128)}), f32[256,1536]{1,0:T(8,128)}) %reduce-scatter.28.cloned.1.call-update) | async-done | bytes 1572880 | tf_op jit(solution)/shard_map/reduce_scatter | solution.py:18
  924.3 109.8 %reduce-scatter.26.cloned.1.call-done = f32[256,1536]{1,0:T(8,128)} async-done(((f32[1024,1536]{1,0:T(8,128)}), f32[256,1536]{1,0:T(8,128)}) %reduce-scatter.26.cloned.1.call-update) | async-done | bytes 1572880 | tf_op jit(solution)/shard_map/reduce_scatter | solution.py:18
  1039.8 64.0 %all-gather.42.cloned.1.call-done = bf16[1024,1536]{1,0:T(8,128)(2,1)} async-done(((bf16[256,1536]{1,0:T(8,128)(2,1)}), bf16[1024,1536]{1,0:T(8,128)(2,1)}) %all-gather.42.cloned.1.call-update) | async-done | bytes 3145744 | tf_op jit(solution)/shard_map/all_gather | solution.py:14
  1133.4 109.5 %reduce-scatter.30.cloned.1.call-done = f32[256,1536]{1,0:T(8,128)} async-done(((f32[1024,1536]{1,0:T(8,128)}), f32[256,1536]{1,0:T(8,128)}) %reduce-scatter.30.cloned.1.call-update) | async-done | bytes 1572880 | tf_op jit(solution)/shard_map/reduce_scatter | solution.py:18
  1321.6 81.1 %while.59 = (s32[]{:T(128)}, f32[2,512,6,64]{1,0,3,2:T(2,128)}, f32[2,1024,6,64]{1,3,2,0:T(8,128)}, f32[2,1024,6,64]{1,3,2,0:T(8,128)}, bf16[2,512,6,64]{1,3,2,0...) while((s32[]{:T(128)}, f32[2,512,6,64]{1,0,3,2:T(2,128)}, ...), condition=%wide.region_28.29_spmd, body=%wide.region_26.28_spmd.sunk | while | flops 2051601408 | bytes 130644152 | solution.py:129
  1484.7 35.5 %all-reduce.4.cloned.1.call-done = bf16[1,130,768]{2,1,0:T(8,128)(2,1)} async-done(((bf16[1,130,768]{2,1,0:T(8,128)(2,1)}), bf16[1,130,768]{2,1,0:T(8,128)(2,1)}) %all-reduce.4.cloned.1.call-update) | async-done | bytes 199696 | tf_op jit(solution)/shard_map/psum | solution.py:274
  1522.1 35.6 %reduce-scatter.54.cloned.1.call-done = bf16[96,384]{1,0:T(8,128)(2,1)} async-done(((bf16[768,384]{1,0:T(8,128)(2,1)}), bf16[96,384]{1,0:T(8,128)(2,1)}) %reduce-scatter.54.cloned.1.call-update) | async-done | bytes 73744
  1559.5 35.5 %reduce-scatter.52.cloned.1.call-done = bf16[96,384]{1,0:T(8,128)(2,1)} async-done(((bf16[768,384]{1,0:T(8,128)(2,1)}), bf16[96,384]{1,0:T(8,128)(2,1)}) %reduce-scatter.52.cloned.1.call-update) | async-done | bytes 73744
  1596.7 38.0 %reduce-scatter.44.cloned.1.call-done = bf16[48,1536]{1,0:T(8,128)(2,1)} async-done(((bf16[384,1536]{1,0:T(8,128)(2,1)}), bf16[48,1536]{1,0:T(8,128)(2,1)}) %reduce-scatter.44.cloned.1.call-update) | async-done | bytes 147472 | tf_op jit(solution)/shard_map/reduce_scatter | solution.py:355
  1636.4 38.3 %reduce-scatter.42.cloned.1.call-done = bf16[192,384]{1,0:T(8,128)(2,1)} async-done(((bf16[1536,384]{1,0:T(8,128)(2,1)}), bf16[192,384]{1,0:T(8,128)(2,1)}) %reduce-scatter.42.cloned.1.call-update) | async-done | bytes 147472 | tf_op jit(solution)/shard_map/reduce_scatter | solution.py:335
  1676.3 38.3 %reduce-scatter.40.cloned.1.call-done = bf16[48,1536]{1,0:T(8,128)(2,1)} async-done(((bf16[384,1536]{1,0:T(8,128)(2,1)}), bf16[48,1536]{1,0:T(8,128)(2,1)}) %reduce-scatter.40.cloned.1.call-update) | async-done | bytes 147472 | tf_op jit(solution)/shard_map/reduce_scatter | solution.py:352
  1716.3 38.1 %reduce-scatter.38.cloned.1.call-done = bf16[192,384]{1,0:T(8,128)(2,1)} async-done(((bf16[1536,384]{1,0:T(8,128)(2,1)}), bf16[192,384]{1,0:T(8,128)(2,1)}) %reduce-scatter.38.cloned.1.call-update) | async-done | bytes 147472 | tf_op jit(solution)/shard_map/reduce_scatter | solution.py:332
  1756.1 38.3 %reduce-scatter.34.cloned.1.call-done = bf16[192,384]{1,0:T(8,128)(2,1)} async-done(((bf16[1536,384]{1,0:T(8,128)(2,1)}), bf16[192,384]{1,0:T(8,128)(2,1)}) %reduce-scatter.34.cloned.1.call-update) | async-done | bytes 147472 | tf_op jit(solution)/shard_map/reduce_scatter | solution.py:326
  1796.1 38.3 %reduce-scatter.36.cloned.1.call-done = bf16[192,384]{1,0:T(8,128)(2,1)} async-done(((bf16[1536,384]{1,0:T(8,128)(2,1)}), bf16[192,384]{1,0:T(8,128)(2,1)}) %reduce-scatter.36.cloned.1.call-update) | async-done | bytes 147472 | tf_op jit(solution)/shard_map/reduce_scatter | solution.py:329
  1836.0 111.3 %reduce-scatter.32.cloned.1.call-done = f32[256,1536]{1,0:T(8,128)} async-done(((f32[1024,1536]{1,0:T(8,128)}), f32[256,1536]{1,0:T(8,128)}) %reduce-scatter.32.cloned.1.call-update) | async-done | bytes 1572880 | tf_op jit(solution)/shard_map/reduce_scatter | solution.py:18
  1949.7 41.7 %all-reduce = (f32[1536]{0:T(1024)}, f32[1536]{0:T(1024)}, f32[1536]{0:T(1024)}, f32[1536]{0:T(1024)}) all-reduce(f32[1536]{0:T(1024)S(1)} %get-tuple-element.406, f32[1536]{0:T(1024)S(1)} %copy-done.58, f32[1536]{0:T(1024)S(1)} %copy-done.56, f32[1536]{0:T(1024)S(1)} %copy-done.57), channel_id=1, replica_groups=mesh['row'=8,'col'=4] {'row','col'}, use_global_device_ids=true, to_apply=%region_38.39 | all-reduce | flops 6144 | bytes 49152 | tf_op jit(solution)/shard_map/psum | solution.py:363
  (429 shorter events, 602.8 us)
Async XLA Ops:
  14.0 280.9 %reduce-scatter.22.cloned.1.call-start = ((), (), s32[]{:S(2)}) async-start(), calls=%async_computation.22 | async-start | bytes 7864320 | tf_op jit(solution)/shard_map/reduce_scatter | solution.py:18
  184.7 203.8 %all-gather.26.cloned.1.call-start = ((), (), s32[]{:S(2)}) async-start(), calls=%async_computation.23 | async-start | bytes 3932160 | tf_op jit(solution)/shard_map/all_gather | solution.py:14
  298.9 231.1 %reduce-scatter.24.cloned.1.call-start = ((), (), s32[]{:S(2)}) async-start(), calls=%async_computation.26 | async-start | bytes 7864320 | tf_op jit(solution)/shard_map/reduce_scatter | solution.py:18
  419.8 216.9 %all-gather.32.cloned.1.call-start = ((), (), s32[]{:S(2)}) async-start(), calls=%async_computation.27 | async-start | bytes 3932160 | tf_op jit(solution)/shard_map/all_gather | solution.py:14
  534.8 206.1 %all-gather.40.cloned.1.call-start = ((), (), s32[]{:S(2)}) async-start(), calls=%async_computation.32 | async-start | bytes 3932160 | tf_op jit(solution)/shard_map/all_gather | solution.py:14
  535.4 244.7 %all-gather.38.cloned.1.call-start = ((), (), s32[]{:S(2)}) async-start(), calls=%async_computation.30 | async-start | bytes 5308416 | tf_op jit(solution)/shard_map/all_gather | solution.py:180
  536.0 384.6 %reduce-scatter.28.cloned.1.call-start = ((), (), s32[]{:S(2)}) async-start(), calls=%async_computation.33 | async-start | bytes 7864320 | tf_op jit(solution)/shard_map/reduce_scatter | solution.py:18
  809.6 224.4 %reduce-scatter.26.cloned.1.call-start = ((), (), s32[]{:S(2)}) async-start(), calls=%async_computation.31 | async-start | bytes 7864320 | tf_op jit(solution)/shard_map/reduce_scatter | solution.py:18
  819.5 284.3 %all-gather.42.cloned.1.call-start = ((), (), s32[]{:S(2)}) async-start(), calls=%async_computation.34 | async-start | bytes 3932160 | tf_op jit(solution)/shard_map/all_gather | solution.py:14
  1039.7 203.2 %reduce-scatter.30.cloned.1.call-start = ((), (), s32[]{:S(2)}) async-start(), calls=%async_computation.35 | async-start | bytes 7864320 | tf_op jit(solution)/shard_map/reduce_scatter | solution.py:18
  1133.3 178.5 %all-gather.44.cloned.1.call-start = ((), (), s32[]{:S(2)}) async-start(), calls=%async_computation.36 | async-start | bytes 3932160 | tf_op jit(solution)/shard_map/all_gather | solution.py:14
  1247.8 215.1 %reduce-scatter.50.cloned.1.call-start = ((), (), s32[]{:S(2)}) async-start(), calls=%async_computation.47 | async-start | bytes 5308416 | tf_op jit(solution)/shard_map/reduce_scatter | solution.py:358
  1257.2 207.9 %reduce-scatter.48.cloned.1.call-start = ((), (), s32[]{:S(2)}) async-start(), calls=%async_computation.46 | async-start | bytes 5308416 | tf_op jit(solution)/shard_map/reduce_scatter | solution.py:347
  1267.9 214.6 %reduce-scatter.46.cloned.1.call-start = ((), (), s32[]{:S(2)}) async-start(), calls=%async_computation.45 | async-start | bytes 5308416 | tf_op jit(solution)/shard_map/reduce_scatter | solution.py:344
  1276.7 243.4 %all-reduce.4.cloned.1.call-start = ((), (), s32[]{:S(2)}) async-start(), calls=%async_computation.38 | async-start | bytes 417792 | tf_op jit(solution)/shard_map/psum | solution.py:274
  1279.7 278.0 %reduce-scatter.54.cloned.1.call-start = ((), (), s32[]{:S(2)}) async-start(), calls=%async_computation.49 | async-start | bytes 663552
  1281.2 313.8 %reduce-scatter.52.cloned.1.call-start = ((), (), s32[]{:S(2)}) async-start(), calls=%async_computation.48 | async-start | bytes 663552
  1282.7 352.1 %reduce-scatter.44.cloned.1.call-start = ((), (), s32[]{:S(2)}) async-start(), calls=%async_computation.44 | async-start | bytes 1327104 | tf_op jit(solution)/shard_map/reduce_scatter | solution.py:355
  1287.1 387.5 %reduce-scatter.42.cloned.1.call-start = ((), (), s32[]{:S(2)}) async-start(), calls=%async_computation.43 | async-start | bytes 1327104 | tf_op jit(solution)/shard_map/reduce_scatter | solution.py:335
  1292.2 422.5 %reduce-scatter.40.cloned.1.call-start = ((), (), s32[]{:S(2)}) async-start(), calls=%async_computation.42 | async-start | bytes 1327104 | tf_op jit(solution)/shard_map/reduce_scatter | solution.py:352
  1321.5 433.0 %reduce-scatter.38.cloned.1.call-start = ((), (), s32[]{:S(2)}) async-start(), calls=%async_computation.41 | async-start | bytes 1327104 | tf_op jit(solution)/shard_map/reduce_scatter | solution.py:332
  1410.1 384.3 %reduce-scatter.34.cloned.1.call-start = ((), (), s32[]{:S(2)}) async-start(), calls=%async_computation.39 | async-start | bytes 1327104 | tf_op jit(solution)/shard_map/reduce_scatter | solution.py:326
  1421.5 412.9 %reduce-scatter.36.cloned.1.call-start = ((), (), s32[]{:S(2)}) async-start(), calls=%async_computation.40 | async-start | bytes 1327104 | tf_op jit(solution)/shard_map/reduce_scatter | solution.py:329
  1427.3 520.0 %reduce-scatter.32.cloned.1.call-start = ((), (), s32[]{:S(2)}) async-start(), calls=%async_computation.37 | async-start | bytes 7864320 | tf_op jit(solution)/shard_map/reduce_scatter | solution.py:18
  (97 other events, 5088.6 us)
Sparse Core Ops, SparseCore 0:
  38.7 63.4 all-gather.15
  184.1 110.7 reduce-scatter.21
  323.8 64.7 all-gather.25
  419.2 110.7 reduce-scatter.23
  531.9 39.2 all-gather.35
  573.2 63.4 all-gather.31
  638.6 37.4 all-gather.33
  677.5 63.4 all-gather.39
  742.7 37.4 all-gather.37
  809.7 110.7 reduce-scatter.27
  922.7 111.2 reduce-scatter.25
  1039.8 63.9 all-gather.41
  1133.4 109.4 reduce-scatter.29
  1247.9 63.9 all-gather.43
  1315.3 52.4 reduce-scatter.49
  1371.2 53.7 reduce-scatter.47
  1428.5 53.9 reduce-scatter.45
  1598.0 36.6 reduce-scatter.43
  1638.0 36.6 reduce-scatter.41
  1677.9 36.6 reduce-scatter.39
  1717.7 36.6 reduce-scatter.37
  1757.7 36.6 reduce-scatter.33
  1797.7 36.6 reduce-scatter.35
  1836.6 110.7 reduce-scatter.31
  (9 shorter events, 247.5 us)
where the time goes:
time: 2010 us; the launch traced here: 2000 us
  waiting for transfers between devices  1520 us (76%)
  matrix products  216 us (11%)
  blocking collectives  88.7 us (4%)
  local copies, waits for them, and re-layouts  83.4 us (4%)
  other arithmetic  75.7 us (4%)
    reduce_scatter x6, waiting for transfers between devices, settle(): lax.psum_scatter(partial_value, 'col', scatter_dimension=0, tiled=True)  651 us
    all_gather x6, waiting for transfers between devices, widen(): return lax.all_gather(narrow, 'col', axis=0, tiled=True)  334 us
    unnamed x35, waiting for transfers between devices  77.6 us
    dot_general x9, matrix products, mixed(): return jnp.dot(left, right, preferred_element_type=jnp.float32)  57.9 us
    psum x1, blocking collectives, local(): lax.psum((first_gain_part, second_gain_part, third_gain_part, down_bias_p...  41.7 us
  transfers between devices with their start and end apart: 33, of which 30 were waited for; matrix products, arithmetic and copies ran while one was open for 14% of the time, Pallas kernels for 0%

commit v1 on v0

v1 whole, which is shorter than its diff:
```python
import jax
import jax.numpy as jnp
from jax import lax
from jax.sharding import PartitionSpec as P


HD = 64
norm_eps = 1e-05
bf16 = jnp.bfloat16
f32 = jnp.float32


def mixed(left, right):
    return jnp.dot(left, right, preferred_element_type=f32)


def mixed_t(left, right):
    return lax.dot_general(left, right, (((1,), (1,)), ((), ())), preferred_element_type=f32)


def outer(left, right):
    return lax.dot_general(left, right, (((0,), (0,)), ((), ())), preferred_element_type=f32)


def norm_forward(stream):
    average = jnp.mean(stream, axis=1, keepdims=True)
    centred = stream - average
    spread = jnp.mean(centred * centred, axis=1, keepdims=True)
    inverse = lax.rsqrt(spread + norm_eps)
    return (centred * inverse, inverse)


def norm_backward(grad_normed, normed, inverse, gain):
    scaled = grad_normed * gain
    first_mean = jnp.mean(scaled, axis=1, keepdims=True)
    second_mean = jnp.mean(scaled * normed, axis=1, keepdims=True)
    grad_stream = inverse * (scaled - first_mean - normed * second_mean)
    return (grad_stream, jnp.sum(grad_normed * normed, axis=0))


def rotate(values, cosine, sine, direction):
    quarter = cosine.shape[-1]
    first = values[..., :quarter]
    second = values[..., quarter : 2 * quarter]
    return jnp.concatenate(
        [
            first * cosine - direction * second * sine,
            second * cosine + direction * first * sine,
            values[..., 2 * quarter :],
        ],
        axis=-1,
    )


def attend(query, key, value, scale):
    scores = jnp.einsum("qhd,khd->hqk", query, key, preferred_element_type=f32) * scale
    row_peak = jnp.max(scores, axis=-1, keepdims=True)
    lifted = jnp.exp(scores - row_peak)
    totals = jnp.sum(lifted, axis=-1, keepdims=True)
    probs = (lifted / totals).astype(bf16)
    result = jnp.einsum("hqk,khd->qhd", probs, value, preferred_element_type=f32)
    return (result.astype(bf16), (row_peak + jnp.log(totals))[..., 0])


def attend_back(query, key, value, grad_block, block_sum, scale):
    scores = jnp.einsum("qhd,khd->hqk", query, key, preferred_element_type=f32) * scale
    probs = jnp.exp(scores - block_sum[..., None])
    grad_probs = jnp.einsum("qhd,khd->hqk", grad_block, value, preferred_element_type=f32)
    weighted = jnp.sum(grad_probs * probs, axis=-1, keepdims=True)
    grad_scores = (probs * (grad_probs - weighted)).astype(bf16)
    grad_query = jnp.einsum("hqk,khd->qhd", grad_scores, key, preferred_element_type=f32) * scale
    grad_key = jnp.einsum("hqk,qhd->khd", grad_scores, query, preferred_element_type=f32) * scale
    grad_value = jnp.einsum(
        "hqk,qhd->khd", probs.astype(bf16), grad_block, preferred_element_type=f32
    )
    return (grad_query, grad_key, grad_value)


def after(value, *others):
    return lax.optimization_barrier((value,) + others)[0]


def column_sums(value):
    ones = lax.optimization_barrier(jnp.full((8, value.shape[0]), 0.125, bf16))
    return jnp.sum(mixed(ones, value), axis=0)


class Line:
    def __init__(self):
        self.mark = ()

    def take(self, *values):
        out = lax.optimization_barrier(tuple(values) + self.mark)[: len(values)]
        return out[0] if len(values) == 1 else out

    def leave(self, *values):
        self.mark = tuple(values)


def make_local(rows, cols):
    ranks = range(cols)
    pairs = rows // 2

    def swap(value, slot):
        return lax.ppermute(value, "col", [(i, i ^ slot) for i in ranks])

    def swap_row(value, slot):
        return lax.ppermute(value, "row", [(i, i ^ slot) for i in range(rows)])

    def spread(value):
        return [value] + [swap(value, k) for k in ranks[1:]]

    def send_back(parts):
        return [parts[0]] + [swap(parts[k].astype(bf16), k) for k in ranks[1:]]

    def add_up(pieces):
        total = pieces[0].astype(f32)
        for piece in pieces[1:]:
            total = total + piece.astype(f32)
        return total

    def reorder(blocks):
        me = lax.axis_index("col")
        stacked = jnp.stack(blocks)
        return [
            lax.dynamic_index_in_dim(stacked, jnp.bitwise_xor(me, j), 0, keepdims=False)
            for j in ranks
        ]

    def sum_over(value, axis, size):
        step = 1
        while step < size:
            hops = [(i, i ^ step) for i in range(size)]
            value = value + lax.ppermute(value, axis, hops)
            step *= 2
        return value

    def widen(value):
        return lax.all_gather(value, "col", axis=0, tiled=True)

    def narrow(value):
        return lax.psum_scatter(value, "col", scatter_dimension=0, tiled=True)

    def gather_one(value):
        return [value] + [swap_row(value, 2 * k) for k in range(1, pairs)]

    def gather_two(received):
        mine = jnp.stack(received)
        return mine, swap_row(mine, 1)

    def gather_three(mine, other, shape, pick=lambda block: block, axis=0):
        row = lax.axis_index("row")
        pair, side = row // 2, row % 2
        out = jnp.zeros(shape, mine.dtype)
        for half, at in ((mine, side), (other, 1 - side)):
            for k in range(pairs):
                block = jnp.expand_dims(pick(half[k]), axis)
                start = [0] * len(shape)
                start[axis] = 2 * jnp.bitwise_xor(pair, k) + at
                out = lax.dynamic_update_slice(out, block, tuple(start))
        return out

    def scatter_one(value):
        side = lax.axis_index("row") % 2
        halves = value.reshape((pairs, 2) + value.shape[1:])
        mine = lax.dynamic_index_in_dim(halves, side, 1, keepdims=False)
        other = lax.dynamic_index_in_dim(halves, 1 - side, 1, keepdims=False)
        return mine, swap_row(other, 1)

    def scatter_two(mine, received):
        half = (mine.astype(f32) + received.astype(f32)).astype(bf16)
        pair = lax.axis_index("row") // 2

        def block(k):
            return lax.dynamic_index_in_dim(half, jnp.bitwise_xor(pair, k), 0, keepdims=False)

        return [block(0)] + [swap_row(block(k), 2 * k) for k in range(1, pairs)]

    def local(
        layer_input,
        context,
        first_gain,
        query_weight,
        key_weight,
        value_weight,
        out_weight,
        second_gain,
        cross_query,
        cross_key,
        cross_value,
        cross_out,
        third_gain,
        gate_weight,
        up_weight,
        gate_bias,
        up_bias,
        down_weight,
        down_bias,
        out_grad,
    ):
        me = lax.axis_index("col")
        width = query_weight.shape[1]
        heads = width // HD
        all_heads = heads * cols
        features = layer_input.shape[1]
        own = layer_input.shape[0]
        tokens = own * cols
        ctx = context[0]
        ctx_len, _ = ctx.shape
        hidden_width = gate_weight.shape[1]
        scale = HD ** (-0.5)
        cq_rows, co_rows = cross_query.shape[0], cross_out.shape[0]
        line = Line()

        def block_of(value, j):
            return lax.slice_in_dim(value, j * own, (j + 1) * own, axis=0)

        def slot_of(value, k):
            return lax.dynamic_slice_in_dim(value, jnp.bitwise_xor(me, k) * own, own, axis=0)

        stream = layer_input.astype(f32)
        normed_one, inverse_one = norm_forward(stream)
        acts_one = (normed_one * first_gain).astype(bf16)
        qkv_shard = jnp.concatenate([query_weight, key_weight, value_weight], axis=1)
        ckv_weight = jnp.concatenate([cross_key, cross_value], axis=1)
        mix_shard = jnp.concatenate([out_weight, ckv_weight.reshape(-1, features)], axis=0)
        gu_shard = jnp.concatenate([gate_weight, up_weight], axis=1)
        cross_shard = jnp.concatenate([cross_query.reshape(-1, features), cross_out], axis=0)
        acts_wide = widen(acts_one)
        qkv_one = gather_one(qkv_shard)
        line.leave(acts_one)
        qkv_two = gather_two(line.take(*qkv_one))
        line.leave(qkv_two[0])
        mix_one = gather_one(line.take(mix_shard))
        gu_one = gather_one(after(line.take(gu_shard), mix_one[1]))
        qkv_cols = gather_three(*line.take(*qkv_two), (rows,) + qkv_shard.shape)
        qkv_cols = qkv_cols.reshape(features, -1)
        line.leave(qkv_cols)
        mix_two = gather_two(line.take(*mix_one))
        line.leave(mix_two[0])
        mix_two = line.take(*mix_two)
        shape = (rows, co_rows, features)
        out_rows = gather_three(*mix_two, shape, lambda block: block[:co_rows])
        out_rows = out_rows.reshape(-1, features)
        shape = (rows, mix_shard.shape[0] - co_rows, features)
        ckv_cols = gather_three(*mix_two, shape, lambda block: block[co_rows:])
        ckv_cols = ckv_cols.reshape(-1, ckv_weight.shape[1])
        ckv = mixed(ctx, ckv_cols).astype(bf16)
        line.leave(ckv, out_rows, ckv_cols)
        ckv_got = spread(ckv)

        quarter = HD // 4
        freqs = 10000.0 ** (-jnp.arange(quarter, dtype=f32) / quarter)
        angles = jnp.arange(tokens, dtype=jnp.int32).astype(f32)[:, None] * freqs[None, :]
        cosine, sine = jnp.cos(angles)[:, None, :], jnp.sin(angles)[:, None, :]
        acts_wide, cosine, sine = line.take(acts_wide, cosine, sine)
        cross_got = spread(after(cross_shard, acts_wide))
        grads_wide = widen(after(out_grad, acts_wide))
        qkv = mixed(acts_wide, qkv_cols)
        split = [qkv[:, j * width : (j + 1) * width].reshape(tokens, heads, HD) for j in range(3)]
        queries = rotate(split[0], cosine, sine, 1.0).astype(bf16)
        keys = rotate(split[1], cosine, sine, 1.0).astype(bf16)
        values = split[2].astype(bf16)
        line.leave(queries, keys, values)
        queries, keys, values = line.take(queries, keys, values)
        results = [None] * cols

        def attend_blocks(js):
            for j in js:
                results[j] = attend(line.take(block_of(queries, j)), keys, values, scale)
                line.leave(*results[j])

        half = cols // 2
        attend_blocks(range(half))
        shards = reorder(line.take(*cross_got))
        cq_shard = jnp.concatenate(
            [shard[:-co_rows].reshape(cq_rows, width) for shard in shards], axis=1
        )
        cross_all = jnp.concatenate([cq_shard] + [shard[-co_rows:] for shard in shards], axis=0)
        line.leave(cross_all)
        cross_one = gather_one(cross_all)
        attend_blocks(range(half, cols))
        self_mixed = jnp.concatenate([r[0] for r in results], axis=0).reshape(tokens, width)
        self_sum = [r[1] for r in results]
        out_value = mixed(line.take(self_mixed), out_rows).astype(bf16)
        line.leave(out_value)
        settled_one = narrow(out_value)

        gu_two = gather_two(line.take(*gu_one))
        line.leave(gu_two[0])
        cross_two = gather_two(line.take(*cross_one))
        line.leave(cross_two[0])
        down_one = gather_one(line.take(down_weight))
        blocks = reorder(line.take(*ckv_got))
        other_keys = jnp.concatenate([b[:, :width] for b in blocks], axis=1)
        other_values = jnp.concatenate([b[:, width:] for b in blocks], axis=1)
        other_keys = other_keys.reshape(ctx_len, all_heads, HD)
        other_values = other_values.reshape(ctx_len, all_heads, HD)
        line.leave(other_keys, other_values)
        cross_two = line.take(*cross_two)
        shape = (rows, cq_rows, features)
        cq_full = gather_three(*cross_two, shape, lambda block: block[:cq_rows])
        cq_full = cq_full.reshape(features, features)
        shape = (cols, rows, co_rows, features)

        def pick(block):
            return block[cq_rows:].reshape(cols, co_rows, features)

        co_full = gather_three(*cross_two, shape, pick, 1).reshape(features, features)
        line.leave(cq_full, co_full)
        gu_cols = gather_three(*line.take(*gu_two), (rows,) + gu_shard.shape)
        gu_cols = gu_cols.reshape(features, -1)
        line.leave(gu_cols)

        stream_one = stream + line.take(settled_one).astype(f32)
        normed_two, inverse_two = norm_forward(stream_one)
        acts_two = (normed_two * second_gain).astype(bf16)
        other_queries = mixed(acts_two, cq_full).astype(bf16).reshape(own, all_heads, HD)
        other_mixed, other_sum = attend(other_queries, other_keys, other_values, scale)
        other_flat = other_mixed.reshape(own, features)
        stream_two = stream_one + mixed(other_flat, co_full)
        normed_three, inverse_three = norm_forward(stream_two)
        acts_three = (normed_three * third_gain).astype(bf16)
        line.leave(acts_three)
        acts_three = widen(acts_three)
        down_two = gather_two(line.take(*down_one))
        line.leave(down_two[0])
        down_rows = gather_three(*line.take(*down_two), (rows,) + down_weight.shape)
        down_rows = down_rows.reshape(-1, features)
        line.leave(down_rows)

        acts_three, grads_wide = line.take(acts_three, grads_wide)
        parts = [None] * cols
        all_hidden = jnp.zeros((tokens, hidden_width), bf16)
        all_grad_gu = jnp.zeros((tokens, 2 * hidden_width), bf16)
        for k in ranks[::-1]:
            acts, grad_slot = line.take(slot_of(acts_three, k), slot_of(grads_wide, k))
            gu = mixed(acts, gu_cols)
            gate = gu[:, :hidden_width] + gate_bias
            upward = gu[:, hidden_width:] + up_bias
            sigmoid_gate = jax.nn.sigmoid(gate)
            silu_gate = gate * sigmoid_gate
            hidden = (silu_gate * upward).astype(bf16)
            grad_hidden = mixed_t(grad_slot, down_rows)
            grad_up = (grad_hidden * silu_gate).astype(bf16)
            grad_gate = (
                grad_hidden * upward * sigmoid_gate * (1.0 + gate * (1.0 - sigmoid_gate))
            ).astype(bf16)
            grad_gu = line.take(jnp.concatenate([grad_gate, grad_up], axis=1))
            parts[k] = mixed_t(grad_gu, gu_cols).astype(bf16)
            line.leave(parts[k])
            here = (jnp.bitwise_xor(me, k) * own, 0)
            all_hidden = lax.dynamic_update_slice(all_hidden, hidden, here)
            all_grad_gu = lax.dynamic_update_slice(all_grad_gu, grad_gu, here)
        three_got = send_back(parts)
        gu_part = outer(acts_three, line.take(all_grad_gu)).astype(bf16)
        line.leave(gu_part)
        gu_one = scatter_one(gu_part.reshape(rows, -1, gu_part.shape[-1]))
        down_part = outer(line.take(all_hidden), grads_wide).astype(bf16)
        line.leave(down_part)
        down_back = scatter_one(down_part.reshape(rows, -1, features))
        down_value = mixed(line.take(all_hidden), down_rows).astype(bf16)
        line.leave(down_value)
        settled_down = narrow(down_value)
        gu_two = scatter_two(*line.take(*gu_one))
        line.leave(gu_two[0])
        down_two = scatter_two(*line.take(*down_back))
        line.leave(down_two[0])

        grad_acts_three = add_up(line.take(*three_got))
        grad_norm_three, third_gain_part = norm_backward(
            grad_acts_three, normed_three, inverse_three, third_gain
        )
        grad_two = out_grad.astype(f32) + grad_norm_three
        grad_two_low = grad_two.astype(bf16)
        grad_other = mixed_t(grad_two_low, co_full).astype(bf16)
        grad_oq, grad_ok, grad_ov = attend_back(
            other_queries,
            other_keys,
            other_values,
            grad_other.reshape(own, all_heads, HD),
            other_sum,
            scale,
        )
        grad_oq = grad_oq.astype(bf16).reshape(own, features)
        grad_acts_two = mixed_t(grad_oq, cq_full)
        grad_norm_two, second_gain_part = norm_backward(
            grad_acts_two, normed_two, inverse_two, second_gain
        )
        grad_one = grad_two + grad_norm_two
        grad_one_low = grad_one.astype(bf16)
        line.leave(grad_one_low, grad_ok, grad_ov)
        grad_one_wide = widen(grad_one_low)

        grad_oq, grad_two_low = line.take(grad_oq, grad_two_low)
        cq_part = outer(acts_two, grad_oq).astype(bf16)
        co_part = outer(other_flat, grad_two_low).astype(bf16)
        co_part = co_part.reshape(cols, rows, -1, features)
        co_part = jnp.moveaxis(co_part, 0, 1).reshape(rows, -1, features)
        cross_part = jnp.concatenate([cq_part.reshape(rows, -1, features), co_part], axis=1)
        line.leave(cross_part)
        cross_back = scatter_one(cross_part)
        gu_bias = column_sums(line.take(all_grad_gu))
        down_bias_part = column_sums(out_grad)
        line.leave(gu_bias, down_bias_part)
        cross_two = scatter_two(*line.take(*cross_back))
        line.leave(cross_two[0])

        def blocks_of(value):
            return [value[:, j * width : (j + 1) * width] for j in ranks]

        grad_one_wide = line.take(grad_one_wide)
        kv_blocks = [
            jnp.concatenate([x, y], axis=1).astype(bf16)
            for x, y in zip(
                blocks_of(grad_ok.reshape(ctx_len, features)),
                blocks_of(grad_ov.reshape(ctx_len, features)),
            )
        ]
        kv_blocks = reorder([after(b, grad_one_wide) for b in kv_blocks])
        kv_got = send_back(kv_blocks)
        grad_self = mixed_t(grad_one_wide, out_rows).astype(bf16).reshape(tokens, heads, HD)
        grad_query, grad_keys, grad_values = [None] * cols, None, None

        def back_blocks(js):
            nonlocal grad_keys, grad_values
            for j in js:
                grad_query[j], gk, gv = attend_back(
                    line.take(block_of(queries, j)),
                    keys,
                    values,
                    block_of(grad_self, j),
                    self_sum[j],
                    scale,
                )
                grad_keys = gk if grad_keys is None else grad_keys + gk
                grad_values = gv if grad_values is None else grad_values + gv
                line.leave(grad_query[j], grad_keys, grad_values)

        back_blocks(range(half))
        grad_ckv = add_up(line.take(*kv_got)).astype(bf16)
        context_part = mixed_t(grad_ckv, ckv_cols).astype(bf16)
        ckv_part = outer(ctx, grad_ckv).astype(bf16)
        line.leave(context_part, ckv_part)
        context_got = spread(context_part)
        back_blocks(range(half, cols))
        grad_query, grad_keys, grad_values = line.take(
            jnp.concatenate(grad_query, axis=0), grad_keys, grad_values
        )
        gq = rotate(grad_query, cosine, sine, -1.0).astype(bf16)
        gk = rotate(grad_keys, cosine, sine, -1.0).astype(bf16)
        gv = grad_values.astype(bf16)
        grad_qkv = jnp.concatenate([v.reshape(tokens, width) for v in (gq, gk, gv)], axis=1)
        part = mixed_t(grad_qkv, qkv_cols).astype(bf16)
        line.leave(part, grad_qkv)
        settled_last = narrow(part)

        qkv_part = outer(acts_wide, line.take(grad_qkv)).astype(bf16)
        line.leave(qkv_part)
        qkv_back = scatter_one(qkv_part.reshape(rows, -1, 3 * width))
        out_part = outer(line.take(self_mixed), grad_one_wide).astype(bf16)
        small_part = jnp.concatenate(
            [out_part.reshape(rows, -1, features), ckv_part.reshape(rows, -1, features)],
            axis=1,
        )
        line.leave(small_part)
        small_back = scatter_one(small_part)
        qkv_two = scatter_two(*line.take(*qkv_back))
        line.leave(qkv_two[0])
        small_two = scatter_two(*line.take(*small_back))
        line.leave(small_two[0])
        cross_half = add_up(line.take(*cross_two)).astype(bf16)
        cq_blocks = blocks_of(cross_half[:cq_rows])
        co_blocks = cross_half[cq_rows:].reshape(cols, co_rows, features)
        cross_blocks = [
            jnp.concatenate([cq_blocks[j].reshape(-1, features), co_blocks[j]], axis=0)
            for j in ranks
        ]
        cross_blocks = reorder(cross_blocks)
        line.leave(*cross_blocks)
        cross_got = send_back(cross_blocks)
        gu_grad = add_up(line.take(*gu_two))
        down_grad = add_up(line.take(*down_two))
        first_gain_part = jnp.sum(part.astype(f32) * acts_wide.astype(f32), axis=0) / first_gain
        sums = jnp.concatenate(
            [first_gain_part, second_gain_part, third_gain_part, down_bias_part, gu_bias]
        )
        line.leave(sums, gu_grad, down_grad)
        sums = sum_over(line.take(sums), "row", rows)
        line.leave(sums)
        qkv_grad = add_up(line.take(*qkv_two))
        small_grad = add_up(line.take(*small_two))
        output_value = (stream_two + line.take(settled_down).astype(f32) + down_bias).astype(bf16)
        line.leave(qkv_grad, small_grad, output_value)

        settled_last, sums = line.take(settled_last, sums)
        gains, gu_bias = sums[: 4 * features], sums[4 * features :]
        gains = sum_over(gains, "col", cols).reshape(4, features)
        grad_norm_one, _ = norm_backward(
            settled_last.astype(f32), normed_one, inverse_one, first_gain
        )
        input_grad = grad_one + grad_norm_one
        context_grad = add_up(reorder(line.take(*context_got)))
        cross_grad = add_up(line.take(*cross_got))
        cross_query_grad = cross_grad[:-co_rows].reshape(cq_rows, width)
        cross_out_grad = cross_grad[-co_rows:]
        ckv_grad = small_grad[co_rows:].reshape(-1, 2 * width)
        return (
            output_value,
            input_grad,
            context_grad[None],
            gains[0],
            qkv_grad[:, :width],
            qkv_grad[:, width : 2 * width],
            qkv_grad[:, 2 * width :],
            small_grad[:co_rows],
            gains[1],
            cross_query_grad,
            ckv_grad[:, :width],
            ckv_grad[:, width:],
            cross_out_grad,
            gains[2],
            gu_grad[:, :hidden_width],
            gu_grad[:, hidden_width:],
            gu_bias[:hidden_width],
            gu_bias[hidden_width:],
            down_grad,
            gains[3],
        )

    return local


def solution(mesh):
    row_col = P("row", "col")
    tokens = P(("row", "col"), None)
    tall = P(("col", "row"), None)
    seqs = P("row", None, None)
    in_specs = (
        tokens,
        seqs,
        P(),
        row_col,
        row_col,
        row_col,
        tall,
        P(),
        row_col,
        row_col,
        row_col,
        tall,
        P(),
        row_col,
        row_col,
        P("col"),
        P("col"),
        tall,
        P(),
        tokens,
    )
    out_specs = (
        tokens,
        tokens,
        seqs,
        P(),
        row_col,
        row_col,
        row_col,
        tall,
        P(),
        row_col,
        row_col,
        row_col,
        tall,
        P(),
        row_col,
        row_col,
        P("col"),
        P("col"),
        tall,
        P(),
    )
    local = make_local(mesh.shape["row"], mesh.shape["col"])

    return jax.shard_map(local, mesh=mesh, in_specs=in_specs, out_specs=out_specs, check_vma=False)
```

time: 2010 us -> 1050 us (0.52)
  waiting for transfers between devices: 1520 us -> 486 us
  blocking collectives: 88.7 us -> 0 us
  local copies, waits for them, and re-layouts: 83.4 us -> 161 us
  starting transfers between devices: 2.88 us -> 73.3 us
  other arithmetic: 75.7 us -> 97.1 us
    reduce_scatter x15 -> x3, waiting for transfers between devices: 896 us -> 0.01 us  [narrow(): return lax.psum_scatter(value, 'col', scatter_dimension=0, tiled=True)]
    all_gather x15 -> x4, waiting for transfers between devices: 509 us -> 129 us  [widen(): return lax.all_gather(value, 'col', axis=0, tiled=True)]
    ppermute x0 -> x63, waiting for transfers between devices: none -> 357 us  [the longest x40 235 us: swap_row(): return lax.ppermute(value, 'row', [(i, i ^ slot) for i in range(rows)])]
    unnamed x35 -> x7, waiting for transfers between devices: 77.6 us -> 0.12 us
    ppermute x0 -> x63, starting transfers between devices: none -> 72.5 us  [the longest x40 40.5 us: swap_row(): return lax.ppermute(value, 'row', [(i, i ^ slot) for i in range(rows)])]
    psum x2 -> x0, blocking collectives: 66.6 us -> none  [the longest x1 41.7 us: local(): lax.psum((first_gain_part, second_gain_part, third_gain_part, down_bias_p...]
    psum x1 -> x0, waiting for transfers between devices: 35.5 us -> none  [local(): lax.psum(context_part.astype(jnp.bfloat16), 'col').astype(jnp.float32)]
    squeeze x0 -> x11, local copies, waits for them, and re-layouts: none -> 22.6 us  [the longest x3 13 us: scatter_one(): other = lax.dynamic_index_in_dim(halves, 1 - side, 1, keepdims=False)]
  transfers between devices with their start and end apart: 33 -> 70, of which waited for: 30 -> 32; matrix products, arithmetic and copies ran while one was open for 14% -> 35% of each run, Pallas kernels for 0% -> 0%
where the time goes in v1:
time: 1050 us; the launch traced here: 1040 us
  waiting for transfers between devices  486 us (46%)
  matrix products  205 us (20%)
  local copies, waits for them, and re-layouts  161 us (15%)
  other arithmetic  97.1 us (9%)
  starting transfers between devices  73.3 us (7%)
  between operations  17.4 us (2%)
    ppermute x40, waiting for transfers between devices, swap_row(): return lax.ppermute(value, 'row', [(i, i ^ slot) for i in range(rows)])  235 us
    all_gather x4, waiting for transfers between devices, widen(): return lax.all_gather(value, 'col', axis=0, tiled=True)  129 us
    ppermute x18, waiting for transfers between devices, swap(): return lax.ppermute(value, 'col', [(i, i ^ slot) for i in ranks])  118 us
    dot_general x13, matrix products, mixed_t(): lax.dot_general(left, right, (((1,), (1,)), ((), ())), preferred_element_...  66.4 us
    dot_general x12, matrix products, mixed(): return jnp.dot(left, right, preferred_element_type=f32)  56.2 us
    dynamic_update_slice x47, local copies, waits for them, and re-layouts, gather_three(): out = lax.dynamic_update_slice(out, block, tuple(start))  48.3 us
    ppermute x40, starting transfers between devices, swap_row(): return lax.ppermute(value, 'row', [(i, i ^ slot) for i in range(rows)])  40.5 us
    dot_general x7, matrix products, outer(): lax.dot_general(left, right, (((0,), (0,)), ((), ())), preferred_element_...  34.3 us
  transfers between devices with their start and end apart: 70, of which 32 were waited for; matrix products, arithmetic and copies ran while one was open for 35% of the time, Pallas kernels for 0%

profile of v1, /device:TPU:0, one launch (start us, length us, event | category | flops | bytes accessed | tf_op | source)
XLA Modules:
  0.0 1040.1 jit_solution(4116419437419456375)
XLA Ops:
  25.2 8.6 collective-permute-done.1
  62.8 55.1 %all-gather.5.cloned.1.call-done = bf16[1024,1536]{1,0:T(8,128)(2,1)} async-done(((bf16[256,1536]{1,0:T(8,128)(2,1)}), bf16[1024,1536]{1,0:T(8,128)(2,1)}) %all-gather.5.cloned.1.call-update) | async-done | bytes 3145744 | tf_op jit(solution)/shard_map/all_gather | solution.py:139
  122.3 7.2 fusion.130
  185.4 23.4 %collective-permute-done.13 = bf16[192,3072]{1,0:T(8,128)(2,1)S(1)} collective-permute-done((bf16[192,3072]{1,0:T(8,128)(2,1)S(1)}, bf16[192,3072]{1,0:T(8,128)(2,1)S(1)}, u32[]{:S(2)}, u32[]{:S(2)}) %collective-permute-start.13) | collective-permute-done | bytes 1179680 | tf_op jit(solution)/shard_map/ppermute | solution.py:108
  210.2 23.9 %collective-permute-done.12 = bf16[192,3072]{1,0:T(8,128)(2,1)S(1)} collective-permute-done((bf16[192,3072]{1,0:T(8,128)(2,1)S(1)}, bf16[192,3072]{1,0:T(8,128)(2,1)S(1)}, u32[]{:S(2)}, u32[]{:S(2)}) %collective-permute-start.12) | collective-permute-done | bytes 1179680 | tf_op jit(solution)/shard_map/ppermute | solution.py:108
  236.6 22.8 %collective-permute-done.17 = bf16[384,1536]{1,0:T(8,128)(2,1)S(1)} collective-permute-done((bf16[384,1536]{1,0:T(8,128)(2,1)S(1)}, bf16[384,1536]{1,0:T(8,128)(2,1)S(1)}, u32[]{:S(2)}, u32[]{:S(2)}) %collective-permute-start.17) | collective-permute-done | bytes 1179680 | tf_op jit(solution)/shard_map/ppermute | solution.py:108
  259.3 23.0 %collective-permute-done.16 = bf16[384,1536]{1,0:T(8,128)(2,1)S(1)} collective-permute-done((bf16[384,1536]{1,0:T(8,128)(2,1)S(1)}, bf16[384,1536]{1,0:T(8,128)(2,1)S(1)}, u32[]{:S(2)}, u32[]{:S(2)}) %collective-permute-start.16) | collective-permute-done | bytes 1179680 | tf_op jit(solution)/shard_map/ppermute | solution.py:108
  296.6 26.4 %collective-permute-done.20 = bf16[130,768]{1,0:T(8,128)(2,1)S(1)} collective-permute-done((bf16[130,768]{1,0:T(8,128)(2,1)S(1)}, bf16[130,768]{1,0:T(8,128)(2,1)S(1)}, u32[]{:S(2)}, u32[]{:S(2)}) %collective-permute-start.20) | collective-permute-done | bytes 199712 | tf_op jit(solution)/shard_map/ppermute | solution.py:105
  411.7 40.0 %all-gather.7.cloned.1.call-done = bf16[1024,1536]{1,0:T(8,128)(2,1)} async-done(((bf16[256,1536]{1,0:T(8,128)(2,1)}), bf16[1024,1536]{1,0:T(8,128)(2,1)}) %all-gather.7.cloned.1.call-update) | async-done | bytes 3145744 | tf_op jit(solution)/shard_map/all_gather | solution.py:139
  465.4 7.2 convolution_convert_fusion.12
  485.1 7.2 convolution_convert_fusion.11
  504.0 7.2 convolution_convert_fusion.10
  525.4 7.2 convolution_convert_fusion.9
  534.5 12.6 %convolution_convert_fusion = bf16[1536,3072]{1,0:T(8,128)(2,1)} fusion(bf16[1024,1536]{1,0:T(8,128)(2,1)S(1)} %copy-done.33, bf16[1024,3072]{1,0:T(8,128)(2,1)S(1)} %constant_dynamic-update-slice_fusion), kind=kOutput, calls=%fused_computation | convolution fusion | flops 9668395008 | bytes 18874368 | tf_op jit(solution)/shard_map/dot_general | solution.py:22
  547.2 8.2 dynamic-slice_bitcast_fusion
  570.5 8.9 convolution_convert_fusion.5
  646.7 33.9 %all-gather.11.cloned.1.call-done = bf16[1024,1536]{1,0:T(8,128)(2,1)} async-done(((bf16[256,1536]{1,0:T(8,128)(2,1)}), bf16[1024,1536]{1,0:T(8,128)(2,1)}) %all-gather.11.cloned.1.call-update) | async-done | bytes 3145744 | tf_op jit(solution)/shard_map/all_gather | solution.py:139
  706.2 14.4 %collective-permute-done.34 = bf16[130,768]{0,1:T(8,128)(2,1)S(1)} collective-permute-done((bf16[130,768]{0,1:T(8,128)(2,1)S(1)}, bf16[130,768]{0,1:T(8,128)(2,1)S(1)}, u32[]{:S(2)}, u32[]{:S(2)}) %collective-permute-start.34) | collective-permute-done | bytes 199712 | tf_op jit(solution)/shard_map/ppermute | solution.py:105
  720.6 50.9 %collective-permute-done.33 = bf16[130,768]{0,1:T(8,128)(2,1)S(1)} collective-permute-done((bf16[130,768]{0,1:T(8,128)(2,1)S(1)}, bf16[130,768]{0,1:T(8,128)(2,1)S(1)}, u32[]{:S(2)}, u32[]{:S(2)}) %collective-permute-start.33) | collective-permute-done | bytes 199712 | tf_op jit(solution)/shard_map/ppermute | solution.py:105
  831.7 21.1 %collective-permute-done.40 = bf16[384,1536]{1,0:T(8,128)(2,1)} collective-permute-done((bf16[384,1536]{1,0:T(8,128)(2,1)}, bf16[384,1536]{1,0:T(8,128)(2,1)}, u32[]{:S(2)}, u32[]{:S(2)}) %collective-permute-start.40) | collective-permute-done | bytes 1179680 | tf_op jit(solution)/shard_map/ppermute | solution.py:108
  855.3 23.0 %collective-permute-done.39 = bf16[384,1536]{1,0:T(8,128)(2,1)} collective-permute-done((bf16[384,1536]{1,0:T(8,128)(2,1)}, bf16[384,1536]{1,0:T(8,128)(2,1)}, u32[]{:S(2)}, u32[]{:S(2)}) %collective-permute-start.39) | collective-permute-done | bytes 1179680 | tf_op jit(solution)/shard_map/ppermute | solution.py:108
  890.8 24.8 %collective-permute-done.44 = bf16[192,1536]{1,0:T(8,128)(2,1)} collective-permute-done((bf16[192,1536]{1,0:T(8,128)(2,1)}, bf16[192,1536]{1,0:T(8,128)(2,1)}, u32[]{:S(2)}, u32[]{:S(2)}) %collective-permute-start.44) | collective-permute-done | bytes 589856 | tf_op jit(solution)/shard_map/ppermute | solution.py:108
  915.6 25.2 %collective-permute-done.43 = bf16[192,1536]{1,0:T(8,128)(2,1)S(1)} collective-permute-done((bf16[192,1536]{1,0:T(8,128)(2,1)}, bf16[192,1536]{1,0:T(8,128)(2,1)S(1)}, u32[]{:S(2)}, u32[]{:S(2)}) %collective-permute-start.43) | collective-permute-done | bytes 589856 | tf_op jit(solution)/shard_map/ppermute | solution.py:108
  1001.2 17.0 %collective-permute-done.61 = bf16[96,1536]{1,0:T(8,128)(2,1)S(1)} collective-permute-done((bf16[96,1536]{1,0:T(8,128)(2,1)}, bf16[96,1536]{1,0:T(8,128)(2,1)S(1)}, u32[]{:S(2)}, u32[]{:S(2)}) %collective-permute-start.61) | collective-permute-done | bytes 294944 | tf_op jit(solution)/shard_map/ppermute | solution.py:105
  (715 shorter events, 523.4 us)
Async XLA Ops:
  7.2 110.7 %all-gather.5.cloned.1.call-start = ((), (), s32[]{:S(2)}) async-start(), calls=%async_computation.3 | async-start | bytes 3932160 | tf_op jit(solution)/shard_map/all_gather | solution.py:139
  53.7 312.8 %reduce-scatter.4.cloned.1.call-start = ((), (), s32[]{:S(2)}) async-start(), calls=%async_computation.4 | async-start | bytes 3932160 | tf_op jit(solution)/shard_map/reduce_scatter | solution.py:142
  177.6 234.2 %all-gather.9.cloned.1.call-start = ((), (), s32[]{:S(2)}) async-start(), calls=%async_computation.6 | async-start | bytes 3932160 | tf_op jit(solution)/shard_map/all_gather | solution.py:139
  182.4 76.9 %collective-permute-start.17 = (bf16[384,1536]{1,0:T(8,128)(2,1)S(1)}, bf16[384,1536]{1,0:T(8,128)(2,1)S(1)}, u32[]{:S(2)}, u32[]{:S(2)}) collective-permute-start(bf16[384,1536]{1,0:T(8,128)(2,1)S(1)} %copy-done.55), channel_id=1, source_target_pairs={{0,24},{4,28},{8,16},{12,20},{16,8},{20,12},{24,0},{28,4},{1,25},{... | collective-permute-start | bytes 3538952 | tf_op jit(solution)/shard_map/ppermute | solution.py:108
  184.8 97.6 %collective-permute-start.16 = (bf16[384,1536]{1,0:T(8,128)(2,1)S(1)}, bf16[384,1536]{1,0:T(8,128)(2,1)S(1)}, u32[]{:S(2)}, u32[]{:S(2)}) collective-permute-start(bf16[384,1536]{1,0:T(8,128)(2,1)S(1)} %copy-done.55), channel_id=1, source_target_pairs={{0,16},{4,20},{8,24},{12,28},{16,0},{20,4},{24,8},{28,12},{1,17},{... | collective-permute-start | bytes 3538952 | tf_op jit(solution)/shard_map/ppermute | solution.py:108
  208.7 73.8 %collective-permute-start.15 = (bf16[384,1536]{1,0:T(8,128)(2,1)S(1)}, bf16[384,1536]{1,0:T(8,128)(2,1)S(1)}, u32[]{:S(2)}, u32[]{:S(2)}) collective-permute-start(bf16[384,1536]{1,0:T(8,128)(2,1)S(1)} %copy-done.55), channel_id=1, source_target_pairs={{0,8},{4,12},{8,0},{12,4},{16,24},{20,28},{24,16},{28,20},{1,9},{5... | collective-permute-start | bytes 3538952 | tf_op jit(solution)/shard_map/ppermute | solution.py:108
  289.4 162.4 %all-gather.7.cloned.1.call-start = ((), (), s32[]{:S(2)}) async-start(), calls=%async_computation.5 | async-start | bytes 3932160 | tf_op jit(solution)/shard_map/all_gather | solution.py:139
  294.9 90.6 %collective-permute-start.24 = (bf16[192,1536]{1,0:T(8,128)(2,1)}, bf16[192,1536]{1,0:T(8,128)(2,1)}, u32[]{:S(2)}, u32[]{:S(2)}) collective-permute-start(bf16[192,1536]{1,0:T(8,128)(2,1)} %param.37), channel_id=1, source_target_pairs={{0,24},{4,28},{8,16},{12,20},{16,8},{20,12},{24,0},{28,4},{1,25},{... | collective-permute-start | bytes 1769480 | tf_op jit(solution)/shard_map/ppermute | solution.py:108
  323.0 62.5 %collective-permute-start.23 = (bf16[192,1536]{1,0:T(8,128)(2,1)}, bf16[192,1536]{1,0:T(8,128)(2,1)}, u32[]{:S(2)}, u32[]{:S(2)}) collective-permute-start(bf16[192,1536]{1,0:T(8,128)(2,1)} %param.37), channel_id=1, source_target_pairs={{0,16},{4,20},{8,24},{12,28},{16,0},{20,4},{24,8},{28,12},{1,17},{... | collective-permute-start | bytes 1769480 | tf_op jit(solution)/shard_map/ppermute | solution.py:108
  324.3 61.2 %collective-permute-start.22 = (bf16[192,1536]{1,0:T(8,128)(2,1)}, bf16[192,1536]{1,0:T(8,128)(2,1)}, u32[]{:S(2)}, u32[]{:S(2)}) collective-permute-start(bf16[192,1536]{1,0:T(8,128)(2,1)} %param.37), channel_id=1, source_target_pairs={{0,8},{4,12},{8,0},{12,4},{16,24},{20,28},{24,16},{28,20},{1,9},{5... | collective-permute-start | bytes 1769480 | tf_op jit(solution)/shard_map/ppermute | solution.py:108
  388.8 291.8 %all-gather.11.cloned.1.call-start = ((), (), s32[]{:S(2)}) async-start(), calls=%async_computation.8 | async-start | bytes 3932160 | tf_op jit(solution)/shard_map/all_gather | solution.py:139
  473.6 118.6 %collective-permute-start.28 = (bf16[256,1536]{1,0:T(8,128)(2,1)}, bf16[256,1536]{1,0:T(8,128)(2,1)}, u32[]{:S(2)}, u32[]{:S(2)}) collective-permute-start(bf16[256,1536]{1,0:T(8,128)(2,1)} %convolution_convert_fusion.12), channel_id=1, source_target_pairs={{0,3},{1,2},{2,1},{3,0},{4,7},{5,6},{6,5},{7,4},{8,11},{9,10},{10,... | collective-permute-start | bytes 2359304 | tf_op jit(solution)/shard_map/ppermute | solution.py:105
  492.5 99.7 %collective-permute-start.27 = (bf16[256,1536]{1,0:T(8,128)(2,1)}, bf16[256,1536]{1,0:T(8,128)(2,1)}, u32[]{:S(2)}, u32[]{:S(2)}) collective-permute-start(bf16[256,1536]{1,0:T(8,128)(2,1)} %convolution_convert_fusion.11), channel_id=1, source_target_pairs={{0,2},{1,3},{2,0},{3,1},{4,6},{5,7},{6,4},{7,5},{8,10},{9,11},{10,... | collective-permute-start | bytes 2359304 | tf_op jit(solution)/shard_map/ppermute | solution.py:105
  511.4 80.8 %collective-permute-start.26 = (bf16[256,1536]{1,0:T(8,128)(2,1)}, bf16[256,1536]{1,0:T(8,128)(2,1)}, u32[]{:S(2)}, u32[]{:S(2)}) collective-permute-start(bf16[256,1536]{1,0:T(8,128)(2,1)} %convolution_convert_fusion.10), channel_id=1, source_target_pairs={{0,1},{1,0},{2,3},{3,2},{4,5},{5,4},{6,7},{7,6},{8,9},{9,8},{10,11... | collective-permute-start | bytes 2359304 | tf_op jit(solution)/shard_map/ppermute | solution.py:105
  618.5 339.4 %reduce-scatter.6.cloned.1.call-start = ((), (), s32[]{:S(2)}) async-start(), calls=%async_computation.7 | async-start | bytes 3932160 | tf_op jit(solution)/shard_map/reduce_scatter | solution.py:142
  632.6 389.4 %reduce-scatter.8.cloned.1.call-start = ((), (), s32[]{:S(2)}) async-start(), calls=%async_computation.9 | async-start | bytes 3932160 | tf_op jit(solution)/shard_map/reduce_scatter | solution.py:142
  699.2 72.3 %collective-permute-start.33 = (bf16[130,768]{0,1:T(8,128)(2,1)S(1)}, bf16[130,768]{0,1:T(8,128)(2,1)S(1)}, u32[]{:S(2)}, u32[]{:S(2)}) collective-permute-start(bf16[130,768]{0,1:T(8,128)(2,1)S(1)} %get-tuple-element.416), channel_id=1, source_target_pairs={{0,2},{1,3},{2,0},{3,1},{4,6},{5,7},{6,4},{7,5},{8,10},{9,11},{10,... | collective-permute-start | bytes 599048 | tf_op jit(solution)/shard_map/ppermute | solution.py:105
  699.5 71.9 %collective-permute-start.32 = (bf16[130,768]{0,1:T(8,128)(2,1)S(1)}, bf16[130,768]{0,1:T(8,128)(2,1)S(1)}, u32[]{:S(2)}, u32[]{:S(2)}) collective-permute-start(bf16[130,768]{0,1:T(8,128)(2,1)S(1)} %get-tuple-element.417), channel_id=1, source_target_pairs={{0,1},{1,0},{2,3},{3,2},{4,5},{5,4},{6,7},{7,6},{8,9},{9,8},{10,11... | collective-permute-start | bytes 599048 | tf_op jit(solution)/shard_map/ppermute | solution.py:105
  810.1 78.8 %collective-permute-start.45 = (bf16[192,1536]{1,0:T(8,128)(2,1)}, bf16[192,1536]{1,0:T(8,128)(2,1)}, u32[]{:S(2)}, u32[]{:S(2)}) collective-permute-start(bf16[192,1536]{1,0:T(8,128)(2,1)} %get-tuple-element.397), channel_id=1, source_target_pairs={{0,24},{4,28},{8,16},{12,20},{16,8},{20,12},{24,0},{28,4},{1,25},{... | collective-permute-start | bytes 1769480 | tf_op jit(solution)/shard_map/ppermute | solution.py:108
  813.1 65.2 %collective-permute-start.39 = (bf16[384,1536]{1,0:T(8,128)(2,1)}, bf16[384,1536]{1,0:T(8,128)(2,1)}, u32[]{:S(2)}, u32[]{:S(2)}) collective-permute-start(bf16[384,1536]{1,0:T(8,128)(2,1)} %get-tuple-element.364), channel_id=1, source_target_pairs={{0,16},{4,20},{8,24},{12,28},{16,0},{20,4},{24,8},{28,12},{1,17},{... | collective-permute-start | bytes 3538952 | tf_op jit(solution)/shard_map/ppermute | solution.py:108
  829.6 86.0 %collective-permute-start.44 = (bf16[192,1536]{1,0:T(8,128)(2,1)}, bf16[192,1536]{1,0:T(8,128)(2,1)}, u32[]{:S(2)}, u32[]{:S(2)}) collective-permute-start(bf16[192,1536]{1,0:T(8,128)(2,1)} %get-tuple-element.398), channel_id=1, source_target_pairs={{0,16},{4,20},{8,24},{12,28},{16,0},{20,4},{24,8},{28,12},{1,17},{... | collective-permute-start | bytes 1769480 | tf_op jit(solution)/shard_map/ppermute | solution.py:108
  852.9 87.9 %collective-permute-start.37 = (bf16[192,3072]{1,0:T(8,128)(2,1)}, bf16[192,3072]{1,0:T(8,128)(2,1)}, u32[]{:S(2)}, u32[]{:S(2)}) collective-permute-start(bf16[192,3072]{1,0:T(8,128)(2,1)} %get-tuple-element.367), channel_id=1, source_target_pairs={{0,24},{4,28},{8,16},{12,20},{16,8},{20,12},{24,0},{28,4},{1,25},{... | collective-permute-start | bytes 3538952 | tf_op jit(solution)/shard_map/ppermute | solution.py:108
  878.2 62.6 %collective-permute-start.36 = (bf16[192,3072]{1,0:T(8,128)(2,1)}, bf16[192,3072]{1,0:T(8,128)(2,1)}, u32[]{:S(2)}, u32[]{:S(2)}) collective-permute-start(bf16[192,3072]{1,0:T(8,128)(2,1)} %get-tuple-element.368), channel_id=1, source_target_pairs={{0,16},{4,20},{8,24},{12,28},{16,0},{20,4},{24,8},{28,12},{1,17},{... | collective-permute-start | bytes 3538952 | tf_op jit(solution)/shard_map/ppermute | solution.py:108
  879.7 61.1 %collective-permute-start.35 = (bf16[192,3072]{1,0:T(8,128)(2,1)}, bf16[192,3072]{1,0:T(8,128)(2,1)}, u32[]{:S(2)}, u32[]{:S(2)}) collective-permute-start(bf16[192,3072]{1,0:T(8,128)(2,1)} %get-tuple-element.369), channel_id=1, source_target_pairs={{0,8},{4,12},{8,0},{12,4},{16,24},{20,28},{24,16},{28,20},{1,9},{5... | collective-permute-start | bytes 3538952 | tf_op jit(solution)/shard_map/ppermute | solution.py:108
  (185 other events, 2350.9 us)
Sparse Core Ops, SparseCore 0:
  53.9 64.0 all-gather.4
  177.7 58.9 reduce-scatter.3
  289.5 67.4 all-gather.8
  388.9 62.7 all-gather.6
  618.6 61.9 all-gather.10
  682.8 84.4 reduce-scatter.5
  820.3 59.6 reduce-scatter.7
